TPU v7x, 128 devices: a whole 4x4x4 slice. The times are simulated.
128 devices in a mesh: row: 8 (over z, core), col: 16 (over y, x).
Axes of the slice: x: 4, y: 4, z: 4, core: 2. Of those that a mesh axis runs over, the one named last changes fastest.
Arguments:
- panel_blocks: bfloat16 [16, 8, 512, 512], P('col', None, 'row'), may hold values from -0.25 to 0.25
- factor_inverse: bfloat16 [16, 512, 512], P('col')
- target_rows: int32 [16, 8], replicated, may hold values from 0 to 15, as said below
- owner_order: int32 [16], replicated, may hold values from 0 to 15, each once
- ancestor_rows: float32 [16, 512, 8192], P('col', 'row'), may hold values from -1.8 to 1.8
Outputs:
- updated_rows: float32 [16, 512, 8192], P('col', 'row')
Inputs may be any that keep to these rules, and one draw needn't show every extreme that they name: `target_rows`: each row names 8 different ancestor block rows in ascending order; each index of col holds exactly one supernode. `owner_order`: each ancestor block row once.
All inputs are finite; a program needn't handle non-finite values.
Results may differ from a plain program's by a relative error of at most 0.0024.
Values may be sent and summed in bfloat16 or wider, within the bound.
A program may use at most 192 MiB of HBM per device.

v0:
```python
import jax
import jax.numpy as jnp
from jax import lax
from jax.sharding import PartitionSpec as P


def solve_rows(blocks, factor_inverse):
    return jnp.einsum(
        "spiw,svw->spiv", blocks, factor_inverse, preferred_element_type=jnp.float32
    ).astype(jnp.bfloat16)


def pick_rows(products, own_targets, order_part):
    matched = own_targets[None, :, :] == order_part[:, None, None]
    places = lax.broadcasted_iota(jnp.int32, matched.shape, 2)
    position = jnp.sum(jnp.where(matched, places, 0), axis=2)
    present = jnp.any(matched, axis=2)
    supernode_ids = lax.broadcasted_iota(jnp.int32, position.shape, 1)
    chosen = products[supernode_ids, position]
    return jnp.where(present[:, :, None, None, None], chosen, jnp.zeros((), chosen.dtype))


def body(panel_blocks, factor_inverse, target_rows, owner_order, ancestor_rows):
    supernodes = panel_blocks.shape[0]
    own_height = panel_blocks.shape[2]
    width = panel_blocks.shape[3]
    ancestors = owner_order.shape[0]
    col_place = lax.axis_index("col")
    own_targets = lax.dynamic_slice_in_dim(target_rows, col_place * supernodes, supernodes, 0)
    own_solved = solve_rows(panel_blocks, factor_inverse)
    products = jnp.einsum(
        "spiw,sqmw->spiqm",
        own_solved,
        lax.all_gather(own_solved, "row", axis=2, tiled=True),
        preferred_element_type=jnp.float32,
    ).astype(jnp.bfloat16)
    block_ids = lax.broadcasted_iota(jnp.int32, (1, 1, 1, ancestors), 3)
    own_onehot = (own_targets[:, :, None] == block_ids[0]).astype(jnp.bfloat16)
    chosen = pick_rows(products, own_targets, owner_order)
    spread = jnp.einsum("sqb,jsiqw->jibw", own_onehot, chosen, preferred_element_type=jnp.float32)
    summed = lax.psum_scatter(
        spread.reshape(
            ancestor_rows.shape[0] * lax.axis_size("col"), own_height, ancestors * width
        ),
        "col",
        scatter_dimension=0,
        tiled=True,
    )
    return ancestor_rows - summed


def solution(mesh):
    return jax.shard_map(
        body,
        mesh=mesh,
        in_specs=(
            P("col", None, "row", None),
            P("col", None, None),
            P(),
            P(),
            P("col", "row", None),
        ),
        out_specs=P("col", "row", None),
        check_vma=False,
    )
```

profile of v0, /device:TPU:1, one launch (start us, length us, event | category | flops | bytes accessed | tf_op | source)
XLA Modules:
  0.0 327.6 jit_solution(10191502747342464816)
XLA Ops:
  6.5 0.0 copy-start
  6.5 0.0 all-gather.3.cloned.1.call-start
  6.5 1.0 copy-done
  7.6 2.3 convolution_convert_fusion
  9.9 0.0 all-gather.3.cloned.1.call-update
  9.9 0.0 reduce-scatter.4.cloned.1.call-start
  10.0 0.9 dynamic-slice_reduce_fusion
  10.8 0.7 fusion.9
  11.6 0.7 compare_reduce_fusion
  12.3 33.7 %all-gather.3.cloned.1.call-done = bf16[8,512,512]{2,1,0:T(8,128)(2,1)} async-done(((bf16[8,64,512]{2,1,0:T(8,128)(2,1)}), bf16[8,512,512]{2,1,0:T(8,128)(2,1)}) %all-gather.3.cloned.1.call-update) | async-done | bytes 4194320 | tf_op jit(solution)/shard_map/all_gather | solution.py:34
  46.1 6.7 %convert_bitcast_fusion = bf16[1,8,64,8,512]{4,2,3,1,0:T(8,128)(2,1)} fusion(bf16[8,512,512]{2,1,0:T(8,128)(2,1)} %all-gather.3.cloned.1.call-done, bf16[8,64,512]{2,1,0:T(8,128)(2,1)} %convolution_convert_fusion), kind=kOutput, calls=%fused_computation.7 | convolution fusion | flops 2149580800 | bytes 8912896 | tf_op jit(solution)/shard_map/spiw,sqmw->spiqm/dot_general | solution.py:31
  52.7 6.9 %gather_fusion = bf16[16,64,8,512]{3,1,2,0:T(8,128)(2,1)} fusion(bf16[1,8,64,8,512]{4,2,3,1,0:T(8,128)(2,1)} %convert_bitcast_fusion, s32[16]{0:T(128)S(1)} %or_bitcast_fusion), kind=kCustom, calls=%fused_computation | custom fusion | bytes 16777344 | tf_op jit(solution)/shard_map/gather | solution.py:19
  59.6 7.2 %fusion = bf16[16,64,8,512]{3,1,2,0:T(8,128)(2,1)} fusion(bf16[16,64,8,512]{3,1,2,0:T(8,128)(2,1)} %gather_fusion, pred[16]{0:T(512)(128)(4,1)S(1)} %compare_reduce_fusion), kind=kLoop, calls=%fused_computation.3 | loop fusion | flops 4194304 | bytes 16777232 | tf_op jit(solution)/shard_map/jit(_where)/select_n | solution.py:20
  66.8 20.6 %convolution_bitcast_fusion = f32[16,64,16,512]{3,2,1,0:T(8,128)} fusion(bf16[16,64,8,512]{3,1,2,0:T(8,128)(2,1)} %fusion, s32[8]{0:T(128)S(1)} %dynamic-slice_reduce_fusion), kind=kOutput, calls=%fused_computation.1 | convolution fusion | flops 134217856 | bytes 41943072 | tf_op jit(solution)/shard_map/sqb,jsiqw->jibw/dot_general | solution.py:40
  87.4 35.9 %reshape.219 = f32[16,64,8192]{2,1,0:T(8,128)} reshape(f32[16,64,16,512]{3,2,1,0:T(8,128)} %convolution_bitcast_fusion) | data formatting | bytes 67108864 | tf_op jit(solution)/shard_map/reshape | solution.py:42
  123.3 0.0 copy-start.2
  123.3 0.0 reduce-scatter.4.cloned.1.call-update
  123.3 0.0 copy-start.1
  123.3 194.3 %reduce-scatter.4.cloned.1.call-done = f32[1,64,8192]{2,1,0:T(8,128)} async-done(((f32[16,64,8192]{2,1,0:T(8,128)}), f32[1,64,8192]{2,1,0:T(8,128)}) %reduce-scatter.4.cloned.1.call-update) | async-done | bytes 2097168
  317.6 0.0 copy-done.2
  317.6 3.1 sub.3
  320.7 0.0 copy-done.1
  (3 shorter events, 0.0 us)
Async XLA Ops:
  6.5 1.0 copy-start
  6.5 39.5 %all-gather.3.cloned.1.call-start = ((), (), s32[]{:S(2)}) async-start(), calls=%async_computation.1 | async-start | bytes 4718592 | tf_op jit(solution)/shard_map/all_gather | solution.py:34
  9.9 307.7 %reduce-scatter.4.cloned.1.call-start = ((), (), s32[]{:S(2)}) async-start(), calls=%async_computation.2 | async-start | bytes 35651584
  123.3 194.3 %copy-start.2 = (f32[1,64,8192]{2,1,0:T(8,128)S(1)}, f32[1,64,8192]{2,1,0:T(8,128)}, u32[]{:S(2)}) copy-start(f32[1,64,8192]{2,1,0:T(8,128)} %param.9) | copy-start | bytes 6291460
  123.3 197.4 %copy-start.1 = (bf16[1,512,512]{2,1,0:T(8,128)(2,1)S(1)}, bf16[1,512,512]{2,1,0:T(8,128)(2,1)}, u32[]{:S(2)}) copy-start(bf16[1,512,512]{2,1,0:T(8,128)(2,1)} %param.6) | copy-start | bytes 1572868
Sparse Core Ops, SparseCore 0:
  10.0 35.9 all-gather.2
  123.4 194.1 reduce-scatter.3
where the time goes:
time: 329 us; the launch traced here: 328 us
  waiting for transfers between devices  228 us (69%)
  local copies, waits for them, and re-layouts  44.7 us (14%)
  matrix products  29.6 us (9%)
  between operations  13.4 us (4%)
  other arithmetic  11.8 us (4%)
    unnamed x3, waiting for transfers between devices  194 us
    reshape x1, local copies, waits for them, and re-layouts, body(): spread.reshape(ancestor_rows.shape[0] * lax.axis_size('col'), own_height,...  35.9 us
    all_gather x1, waiting for transfers between devices, body(): lax.all_gather(own_solved, 'row', axis=2, tiled=True)  33.7 us
    dot_general x1, matrix products, body(): jnp.einsum('sqb,jsiqw->jibw', own_onehot, chosen, preferred_element_type=...  20.6 us
    select_n x1, other arithmetic, pick_rows(): jnp.where(present[:, :, None, None, None], chosen, jnp.zeros((), chosen.d...  7.19 us
    gather x1, local copies, waits for them, and re-layouts, pick_rows(): chosen = products[supernode_ids, position]  6.87 us
    dot_general x1, matrix products, body(): jnp.einsum('spiw,sqmw->spiqm', own_solved, lax.all_gather(own_solved, 'ro...  6.66 us
  transfers between devices with their start and end apart: 2, of which 2 were waited for; matrix products, arithmetic and copies ran while one was open for 1% of the time, Pallas kernels for 0%

commit v1 on v0

--- a/solution.py
+++ b/solution.py
@@ -2,6 +2,7 @@
 import jax.numpy as jnp
 from jax import lax
 from jax.sharding import PartitionSpec as P
+from jax.lax import axis_index, axis_size, ppermute
 
 
 def solve_rows(blocks, factor_inverse):
@@ -21,6 +22,23 @@
 
 
 def body(panel_blocks, factor_inverse, target_rows, owner_order, ancestor_rows):
+
+    def start_screen(buf):
+        mesh_name = "row"
+        n_all = axis_size(mesh_name)
+        rows = [(num, (num + 1) % n_all) for num in range(n_all)]
+        found = [(num, (num - 1) % n_all) for num in range(n_all)]
+        u1, latest = ([buf], [buf])
+        for _ in range(n_all // 2):
+            far_arr = ppermute(u1[-1], axis_name=mesh_name, perm=rows)
+            u1.append(far_arr)
+        for _ in range((n_all - 1) // 2):
+            current_value = ppermute(latest[-1], perm=found, axis_name=mesh_name)
+            latest.append(current_value)
+        step_out = jnp.concatenate([*u1[::-1], *latest[1:]], 2)
+        state_now = axis_index(mesh_name)
+        return jnp.roll(step_out, shift=(state_now - n_all // 2) * buf.shape[2], axis=2)
+
     supernodes = panel_blocks.shape[0]
     own_height = panel_blocks.shape[2]
     width = panel_blocks.shape[3]
@@ -29,10 +47,7 @@
     own_targets = lax.dynamic_slice_in_dim(target_rows, col_place * supernodes, supernodes, 0)
     own_solved = solve_rows(panel_blocks, factor_inverse)
     products = jnp.einsum(
-        "spiw,sqmw->spiqm",
-        own_solved,
-        lax.all_gather(own_solved, "row", axis=2, tiled=True),
-        preferred_element_type=jnp.float32,
+        "spiw,sqmw->spiqm", own_solved, start_screen(own_solved), preferred_element_type=jnp.float32
     ).astype(jnp.bfloat16)
     block_ids = lax.broadcasted_iota(jnp.int32, (1, 1, 1, ancestors), 3)
     own_onehot = (own_targets[:, :, None] == block_ids[0]).astype(jnp.bfloat16)

time: 329 us -> 335 us (1.018)
  starting transfers between devices: 0.04 us -> 14.3 us
  waiting for transfers between devices: 228 us -> 221 us
    all_gather x1 -> x0, waiting for transfers between devices: 33.7 us -> none  [body(): lax.all_gather(own_solved, 'row', axis=2, tiled=True)]
    ppermute x0 -> x7, waiting for transfers between devices: none -> 21.7 us  [the longest x4 17.1 us: start_screen(): far_arr = ppermute(u1[-1], axis_name=mesh_name, perm=rows)]
    ppermute x0 -> x7, starting transfers between devices: none -> 14.3 us  [the longest x4 10.5 us: start_screen(): far_arr = ppermute(u1[-1], axis_name=mesh_name, perm=rows)]
    unnamed x3 -> x2, waiting for transfers between devices: 194 us -> 199 us
  transfers between devices with their start and end apart: 2 -> 8, of which waited for: 2 -> 7; matrix products, arithmetic and copies ran while one was open for 1% -> 1% of each run, Pallas kernels for 0% -> 0%
where the time goes in v1:
time: 335 us; the launch traced here: 334 us
  waiting for transfers between devices  221 us (66%)
  local copies, waits for them, and re-layouts  47.3 us (14%)
  matrix products  26.6 us (8%)
  starting transfers between devices  14.3 us (4%)
  between operations  13.5 us (4%)
  other arithmetic  11.8 us (4%)
    unnamed x2, waiting for transfers between devices  199 us
    reshape x1, local copies, waits for them, and re-layouts, body(): spread.reshape(ancestor_rows.shape[0] * lax.axis_size('col'), own_height,...  35.9 us
    dot_general x1, matrix products, body(): jnp.einsum('sqb,jsiqw->jibw', own_onehot, chosen, preferred_element_type=...  20.6 us
    ppermute x4, waiting for transfers between devices, start_screen(): far_arr = ppermute(u1[-1], axis_name=mesh_name, perm=rows)  17.1 us
    ppermute x4, starting transfers between devices, start_screen(): far_arr = ppermute(u1[-1], axis_name=mesh_name, perm=rows)  10.5 us
    select_n x1, other arithmetic, pick_rows(): jnp.where(present[:, :, None, None, None], chosen, jnp.zeros((), chosen.d...  7.2 us
    gather x1, local copies, waits for them, and re-layouts, pick_rows(): chosen = products[supernode_ids, position]  6.87 us
  transfers between devices with their start and end apart: 8, of which 7 were waited for; matrix products, arithmetic and copies ran while one was open for 1% of the time, Pallas kernels for 0%

profile of v1, /device:TPU:1, one launch (start us, length us, event | category | flops | bytes accessed | tf_op | source)
XLA Modules:
  0.0 334.1 jit_solution(1745991704207586773)
XLA Ops:
  6.5 0.0 copy-start
  6.5 0.0 reduce-scatter.4.cloned.1.call-start
  6.5 1.0 copy-done
  7.6 1.5 convolution_convert_fusion
  9.1 3.0 collective-permute-start
  12.1 6.1 %collective-permute-done = bf16[1,8,64,512]{3,2,1,0:T(8,128)(2,1)S(1)} collective-permute-done((bf16[1,8,64,512]{3,2,1,0:T(8,128)(2,1)S(1)}, bf16[1,8,64,512]{3,2,1,0:T(8,128)(2,1)S(1)}, u32[]{:S(2)}, u32[]{:S(2)}) %collective-permute-start) | collective-permute-done | bytes 524320 | tf_op jit(solution)/shard_map/ppermute | solution.py:33
  18.3 2.5 collective-permute-start.1
  20.7 0.2 collective-permute-start.4
  21.0 5.9 %collective-permute-done.1 = bf16[1,8,64,512]{3,2,1,0:T(8,128)(2,1)S(1)} collective-permute-done((bf16[1,8,64,512]{3,2,1,0:T(8,128)(2,1)S(1)}, bf16[1,8,64,512]{3,2,1,0:T(8,128)(2,1)S(1)}, u32[]{:S(2)}, u32[]{:S(2)}) %collective-permute-start.1) | collective-permute-done | bytes 524320 | tf_op jit(solution)/shard_map/ppermute | solution.py:33
  26.9 2.5 collective-permute-start.2
  29.3 0.9 dynamic-slice_reduce_fusion
  30.2 0.7 fusion.10
  31.0 0.0 collective-permute-done.4
  31.0 1.4 collective-permute-start.5
  32.4 3.1 collective-permute-done.2
  35.5 2.5 collective-permute-start.3
  38.0 0.7 compare_reduce_fusion
  38.7 1.2 collective-permute-done.5
  39.9 2.2 collective-permute-start.6
  42.0 2.0 collective-permute-done.3
  44.1 1.1 constant_dynamic-update-slice_fusion.15
  45.4 3.5 %collective-permute-done.6 = bf16[1,8,64,512]{3,2,1,0:T(8,128)(2,1)S(1)} collective-permute-done((bf16[1,8,64,512]{3,2,1,0:T(8,128)(2,1)S(1)}, bf16[1,8,64,512]{3,2,1,0:T(8,128)(2,1)S(1)}, u32[]{:S(2)}, u32[]{:S(2)}) %collective-permute-start.6) | collective-permute-done | bytes 524320 | tf_op jit(solution)/shard_map/ppermute | solution.py:36
  48.9 1.1 constant_dynamic-update-slice_fusion.7
  50.3 4.4 %convert_bitcast_fusion = bf16[1,8,64,8,512]{4,2,3,1,0:T(8,128)(2,1)} fusion(bf16[1,8,1024,512]{3,2,1,0:T(8,128)(2,1)S(1)} %constant_dynamic-update-slice_fusion, s32[]{:T(128)S(6)} %select_n.64, bf16[8,64,512]{2,1,0:T(8,128)(2,1)S(1)} %convolution_convert_fusion), kind=kOutput, calls=%fused_computation.7 | convolution fusion | flops 2149580800 | bytes 8912900 | tf_op jit(solution)/shard_map/spiw,sqmw->spiqm/dot_general | solution.py:49
  54.8 6.9 %gather_fusion = bf16[16,64,8,512]{3,1,2,0:T(8,128)(2,1)} fusion(bf16[1,8,64,8,512]{4,2,3,1,0:T(8,128)(2,1)} %convert_bitcast_fusion, s32[16]{0:T(128)S(1)} %or_bitcast_fusion), kind=kCustom, calls=%fused_computation | custom fusion | bytes 16777344 | tf_op jit(solution)/shard_map/gather | solution.py:20
  61.6 7.2 %fusion = bf16[16,64,8,512]{3,1,2,0:T(8,128)(2,1)} fusion(bf16[16,64,8,512]{3,1,2,0:T(8,128)(2,1)} %gather_fusion, pred[16]{0:T(512)(128)(4,1)S(1)} %compare_reduce_fusion), kind=kLoop, calls=%fused_computation.3 | loop fusion | flops 4194304 | bytes 16777232 | tf_op jit(solution)/shard_map/jit(_where)/select_n | solution.py:21
  68.8 20.6 %convolution_bitcast_fusion = f32[16,64,16,512]{3,2,1,0:T(8,128)} fusion(bf16[16,64,8,512]{3,1,2,0:T(8,128)(2,1)} %fusion, s32[8]{0:T(128)S(1)} %dynamic-slice_reduce_fusion), kind=kOutput, calls=%fused_computation.1 | convolution fusion | flops 134217856 | bytes 41943072 | tf_op jit(solution)/shard_map/sqb,jsiqw->jibw/dot_general | solution.py:55
  89.5 35.9 %reshape.219 = f32[16,64,8192]{2,1,0:T(8,128)} reshape(f32[16,64,16,512]{3,2,1,0:T(8,128)} %convolution_bitcast_fusion) | data formatting | bytes 67108864 | tf_op jit(solution)/shard_map/reshape | solution.py:57
  125.3 0.0 reduce-scatter.4.cloned.1.call-update
  125.4 0.0 copy-start.1
  125.4 198.8 %reduce-scatter.4.cloned.1.call-done = f32[1,64,8192]{2,1,0:T(8,128)} async-done(((f32[16,64,8192]{2,1,0:T(8,128)}), f32[1,64,8192]{2,1,0:T(8,128)}) %reduce-scatter.4.cloned.1.call-update) | async-done | bytes 2097168
  324.1 3.1 sub.12
  (20 shorter events, 0.5 us)
Async XLA Ops:
  6.5 1.0 copy-start
  6.5 317.6 %reduce-scatter.4.cloned.1.call-start = ((), (), s32[]{:S(2)}) async-start(), calls=%async_computation.1 | async-start | bytes 35651584
  9.1 9.2 %collective-permute-start = (bf16[1,8,64,512]{3,2,1,0:T(8,128)(2,1)S(1)}, bf16[1,8,64,512]{3,2,1,0:T(8,128)(2,1)S(1)}, u32[]{:S(2)}, u32[]{:S(2)}) collective-permute-start(bf16[1,8,64,512]{3,2,1,0:T(8,128)(2,1)S(1)} %bitcast.47), channel_id=1, source_target_pairs={{0,16},{16,32},{32,48},{48,64},{64,80},{80,96},{96,112},{112,0},{1... | collective-permute-start | bytes 1572872 | tf_op jit(solution)/shard_map/ppermute | solution.py:33
  18.3 8.6 %collective-permute-start.1 = (bf16[1,8,64,512]{3,2,1,0:T(8,128)(2,1)S(1)}, bf16[1,8,64,512]{3,2,1,0:T(8,128)(2,1)S(1)}, u32[]{:S(2)}, u32[]{:S(2)}) collective-permute-start(bf16[1,8,64,512]{3,2,1,0:T(8,128)(2,1)S(1)} %collective-permute-done), channel_id=1, source_target_pairs={{0,16},{16,32},{32,48},{48,64},{64,80},{80,96},{96,112},{112,0},{1... | collective-permute-start | bytes 1572872 | tf_op jit(solution)/shard_map/ppermute | solution.py:33
  20.7 10.2 %collective-permute-start.4 = (bf16[1,8,64,512]{3,2,1,0:T(8,128)(2,1)S(1)}, bf16[1,8,64,512]{3,2,1,0:T(8,128)(2,1)S(1)}, u32[]{:S(2)}, u32[]{:S(2)}) collective-permute-start(bf16[1,8,64,512]{3,2,1,0:T(8,128)(2,1)S(1)} %bitcast.48), channel_id=1, source_target_pairs={{0,112},{16,0},{32,16},{48,32},{64,48},{80,64},{96,80},{112,96},{1... | collective-permute-start | bytes 1572872 | tf_op jit(solution)/shard_map/ppermute | solution.py:36
  26.9 8.6 %collective-permute-start.2 = (bf16[1,8,64,512]{3,2,1,0:T(8,128)(2,1)S(1)}, bf16[1,8,64,512]{3,2,1,0:T(8,128)(2,1)S(1)}, u32[]{:S(2)}, u32[]{:S(2)}) collective-permute-start(bf16[1,8,64,512]{3,2,1,0:T(8,128)(2,1)S(1)} %collective-permute-done.1), channel_id=1, source_target_pairs={{0,16},{16,32},{32,48},{48,64},{64,80},{80,96},{96,112},{112,0},{1... | collective-permute-start | bytes 1572872 | tf_op jit(solution)/shard_map/ppermute | solution.py:33
  31.0 8.9 %collective-permute-start.5 = (bf16[1,8,64,512]{3,2,1,0:T(8,128)(2,1)S(1)}, bf16[1,8,64,512]{3,2,1,0:T(8,128)(2,1)S(1)}, u32[]{:S(2)}, u32[]{:S(2)}) collective-permute-start(bf16[1,8,64,512]{3,2,1,0:T(8,128)(2,1)S(1)} %collective-permute-done.4), channel_id=1, source_target_pairs={{0,112},{16,0},{32,16},{48,32},{64,48},{80,64},{96,80},{112,96},{1... | collective-permute-start | bytes 1572872 | tf_op jit(solution)/shard_map/ppermute | solution.py:36
  35.5 8.6 %collective-permute-start.3 = (bf16[1,8,64,512]{3,2,1,0:T(8,128)(2,1)S(1)}, bf16[1,8,64,512]{3,2,1,0:T(8,128)(2,1)}, u32[]{:S(2)}, u32[]{:S(2)}) collective-permute-start(bf16[1,8,64,512]{3,2,1,0:T(8,128)(2,1)S(1)} %collective-permute-done.2), channel_id=1, source_target_pairs={{0,16},{16,32},{32,48},{48,64},{64,80},{80,96},{96,112},{112,0},{1... | collective-permute-start | bytes 1572872 | tf_op jit(solution)/shard_map/ppermute | solution.py:33
  39.9 9.0 %collective-permute-start.6 = (bf16[1,8,64,512]{3,2,1,0:T(8,128)(2,1)S(1)}, bf16[1,8,64,512]{3,2,1,0:T(8,128)(2,1)S(1)}, u32[]{:S(2)}, u32[]{:S(2)}) collective-permute-start(bf16[1,8,64,512]{3,2,1,0:T(8,128)(2,1)S(1)} %collective-permute-done.5), channel_id=1, source_target_pairs={{0,112},{16,0},{32,16},{48,32},{64,48},{80,64},{96,80},{112,96},{1... | collective-permute-start | bytes 1572872 | tf_op jit(solution)/shard_map/ppermute | solution.py:36
  125.3 198.8 %copy-start.2 = (f32[1,64,8192]{2,1,0:T(8,128)S(1)}, f32[1,64,8192]{2,1,0:T(8,128)}, u32[]{:S(2)}) copy-start(f32[1,64,8192]{2,1,0:T(8,128)} %param.9) | copy-start | bytes 6291460
  125.4 201.9 %copy-start.1 = (bf16[1,512,512]{2,1,0:T(8,128)(2,1)S(1)}, bf16[1,512,512]{2,1,0:T(8,128)(2,1)}, u32[]{:S(2)}) copy-start(bf16[1,512,512]{2,1,0:T(8,128)(2,1)} %param.6) | copy-start | bytes 1572868
Sparse Core Ops, SparseCore 0:
  125.5 198.6 reduce-scatter.3
